TPU v7x, 32 devices: a whole 2x2x4 slice. The times are simulated.
32 devices in a mesh: dp: 4 (over z), expert: 8 (over y, x, core).
Axes of the slice: x: 2, y: 2, z: 4, core: 2. Of those that a mesh axis runs over, the one named last changes fastest.
Arguments:
- out_grad: bfloat16 [8192, 4096], P(('dp', 'expert')), may hold values from -6 to 6
- destination: int32 [8192, 1], P(('dp', 'expert')), may hold values from 0 to 7; in each aligned block of 256 rows (0 to 255, 256 to 511, ...) at most 64 rows name the same one
- hidden: bfloat16 [16384, 1024], P(('dp', 'expert')), may hold values from -6 to 6
- weight: bfloat16 [8, 1024, 4096], P('expert', None, 'dp'), may hold values from -0.09375 to 0.09375
- left_prev: float32 [8, 2048, 1024], P('expert', 'dp'), may hold values from -3 to 3
- right_prev: float32 [8, 4096, 2048], P('expert', 'dp'), may hold values from -3 to 3
Outputs:
- grad_rows: bfloat16 [8192, 1024], P(('dp', 'expert'))
- left_stats: float32 [8, 2048, 1024], P('expert', 'dp')
- right_stats: float32 [8, 4096, 2048], P('expert', 'dp')
Inputs may be any that keep to these rules, and one draw needn't show every extreme that they name: Among the rows of one device at most 64 have the same destination, and on some device that many do.
All inputs are finite; a program needn't handle non-finite values.
Results may differ from a plain program's by a relative error of at most 0.001.
Values may be sent and summed in bfloat16 or wider, within the bound.
A program may use at most 128 MiB of HBM per device.

v0:
```python
import jax
import jax.numpy as jnp
from jax import lax
from jax.sharding import PartitionSpec as P

ema_decay = 0.9


def swapped(value, axis, distance):
    mask = 2**distance
    pairs = [(source, source ^ mask) for source in range(lax.axis_size(axis))]
    return lax.ppermute(value, axis, pairs)


def slot_places(dest_column, expert_count, capacity):
    choose = (dest_column[:, None] == jnp.arange(expert_count, dtype=jnp.int32)[None, :]).astype(
        jnp.int32
    )
    before = jnp.cumsum(choose, axis=0) - choose
    slot_rank = jnp.sum(before * choose, axis=1)
    return dest_column * capacity + slot_rank


def local(out_grad, destination, hidden, weight, left_prev, right_prev):
    expert_count = lax.axis_size("expert")
    group_count = lax.axis_size("dp")
    row_count, model_width = out_grad.shape
    slot_count, hidden_width = hidden.shape
    capacity = slot_count // expert_count
    target_slots = slot_places(destination[:, 0], expert_count, capacity)
    outgoing = jnp.zeros((slot_count, model_width), out_grad.dtype).at[target_slots].set(out_grad)
    arrived = lax.all_to_all(
        outgoing.reshape(expert_count, capacity, model_width),
        "expert",
        split_axis=0,
        concat_axis=0,
        tiled=True,
    )
    arrived = arrived.reshape(slot_count, model_width)
    columns = arrived
    slot_grad = lax.dot_general(
        columns,
        lax.all_gather(weight[0], "dp", axis=1, tiled=True),
        (((1,), (1,)), ((), ())),
        preferred_element_type=jnp.float32,
    ).astype(jnp.bfloat16)
    returned = lax.all_to_all(
        slot_grad.reshape(expert_count, capacity, hidden_width),
        "expert",
        split_axis=0,
        concat_axis=0,
        tiled=True,
    )
    grad_rows = returned.reshape(slot_count, hidden_width)[target_slots]
    half_width = model_width // group_count
    block_width = 2 * half_width
    columns_all = lax.all_to_all(arrived, "dp", split_axis=1, concat_axis=0, tiled=True)
    columns = columns_all
    own_piece = lax.dot_general(
        columns,
        lax.all_gather(hidden, "dp", axis=0, tiled=True),
        (((0,), (0,)), ((), ())),
        preferred_element_type=jnp.float32,
    )
    partner = swapped(own_piece.astype(jnp.bfloat16), "dp", 0).astype(own_piece.dtype)
    parity = lax.axis_index("dp") % 2
    upper_half = parity == 0
    first_half = jnp.where(upper_half, own_piece, partner)
    second_half = jnp.where(upper_half, partner, own_piece)
    block_grad = jnp.concatenate([first_half, second_half], axis=0)
    scale_left = 1.0 / (group_count * row_count * block_width)
    scale_right = 1.0 / (group_count * row_count * hidden_width)
    right_gram = (
        lax.dot_general(
            own_piece,
            block_grad,
            (((1,), (1,)), ((), ())),
            precision=lax.Precision.HIGHEST,
            preferred_element_type=jnp.float32,
        )
        * scale_right
    )
    half_hidden = hidden_width // 2
    hidden_cols = lax.dynamic_slice_in_dim(block_grad, parity * half_hidden, half_hidden, 1)
    left_gram = (
        lax.dot_general(
            hidden_cols,
            block_grad,
            (((0,), (0,)), ((), ())),
            precision=lax.Precision.HIGHEST,
            preferred_element_type=jnp.float32,
        )
        * scale_left
    )
    left_stats = ema_decay * left_prev + (1.0 - ema_decay) * left_gram[None]
    right_stats = ema_decay * right_prev + (1.0 - ema_decay) * right_gram[None]
    return (grad_rows, left_stats, right_stats)


def solution(mesh):
    placed = (
        P(("dp", "expert"), None),
        P(("dp", "expert"), None),
        P(("dp", "expert"), None),
        P("expert", None, "dp"),
        P("expert", "dp", None),
        P("expert", "dp", None),
    )
    return jax.shard_map(
        local,
        mesh=mesh,
        in_specs=placed,
        out_specs=(P(("dp", "expert"), None), P("expert", "dp", None), P("expert", "dp", None)),
        check_vma=False,
    )
```

profile of v0, /device:TPU:1, one launch (start us, length us, event | category | flops | bytes accessed | tf_op | source)
XLA Modules:
  0.0 439.9 jit_solution(14873368726343647602)
XLA Ops:
  7.2 0.0 all-gather.4.cloned.1.call-start
  7.2 0.7 all-gather.4.cloned.1.call-update
  7.9 0.7 fusion.15
  8.6 0.6 reduce-window.6
  9.2 0.2 slice_reduce_fusion
  9.4 0.8 fusion.14
  10.2 0.7 compare_select_fusion
  10.9 7.1 %scatter_custom_fusion = bf16[512,4096]{1,0:T(8,128)(2,1)} fusion(s32[256]{0:T(256)S(1)} %bitcast.37, bf16[256,4096]{1,0:T(8,128)(2,1)} %param.6, bf16[]{:T(256)} %constant.14.clone.1), kind=kCustom, calls=%fused_computation.14 | custom fusion | bytes 4194816 | tf_op jit(solution)/shard_map/scatter | solution.py:31
  18.0 5.2 %all-to-all-start = ((bf16[8,64,4096]{2,1,0:T(8,128)(2,1)}), bf16[8,64,4096]{2,1,0:T(8,128)(2,1)}, u32[]{:S(2)}, u32[]{:S(2)}) async-start(bf16[8,64,4096]{2,1,0:T(8,128)(2,1)} %bitcast.34), calls=%async_computation | async-start | bytes 8388608 | tf_op jit(solution)/shard_map/all_to_all | solution.py:32
  23.2 0.0 all-gather.6.cloned.1.call-start
  23.2 0.7 all-gather.6.cloned.1.call-update
  23.9 44.9 %all-to-all-done = bf16[8,64,4096]{2,1,0:T(8,128)(2,1)} async-done(((bf16[8,64,4096]{2,1,0:T(8,128)(2,1)}), bf16[8,64,4096]{2,1,0:T(8,128)(2,1)}, u32[]{:S(2)}, u32[]{:S(2)}) %all-to-all-start) | async-done | bytes 4194336 | tf_op jit(solution)/shard_map/all_to_all | solution.py:32
  68.9 7.8 %all_to_all.22 = bf16[512,4,1024]{2,1,0:T(4,128)(2,1)} reshape(bf16[8,64,4096]{2,1,0:T(8,128)(2,1)} %all-to-all-done) | data formatting | bytes 8388608 | tf_op jit(solution)/shard_map/all_to_all | solution.py:57
  76.7 5.5 %copy.10 = bf16[512,4,1024]{2,0,1:T(8,128)(2,1)} copy(bf16[512,4,1024]{2,1,0:T(4,128)(2,1)} %all_to_all.22) | data formatting | bytes 8388608 | tf_op jit(solution)/shard_map/all_to_all | solution.py:57
  82.2 5.8 %all-to-all-start.2 = ((bf16[512,4,1024]{2,0,1:T(8,128)(2,1)}), bf16[512,4,1024]{2,0,1:T(8,128)(2,1)}, u32[]{:S(2)}, u32[]{:S(2)}) async-start(bf16[512,4,1024]{2,0,1:T(8,128)(2,1)} %copy.10), calls=%async_computation.2 | async-start | bytes 8388608 | tf_op jit(solution)/shard_map/all_to_all | solution.py:57
  88.0 4.2 all-gather.4.cloned.1.call-done
  92.2 194.6 %all-to-all-done.2 = bf16[512,4,1024]{2,0,1:T(8,128)(2,1)} async-done(((bf16[512,4,1024]{2,0,1:T(8,128)(2,1)}), bf16[512,4,1024]{2,0,1:T(8,128)(2,1)}, u32[]{:S(2)}, u32[]{:S(2)}) %all-to-all-start.2) | async-done | bytes 4194336 | tf_op jit(solution)/shard_map/all_to_all | solution.py:57
  286.8 10.7 %fusion.19 = (bf16[1024,1024]{1,0:T(8,128)(2,1)}, f32[1024,1024]{1,0:T(8,128)}) fusion(bf16[2048,1024]{1,0:T(8,128)(2,1)} %bitcast.12, bf16[2048,1024]{1,0:T(8,128)(2,1)} %all-gather.4.cloned.1.call-done), kind=kOutput, calls=%fused_computation.29 | convolution fusion | flops 4296015872 | bytes 14680064 | tf_op jit(solution)/shard_map/dot_general | solution.py:59
  297.5 0.0 collective-permute-start
  297.5 60.1 %collective-permute-done = bf16[1024,1024]{1,0:T(8,128)(2,1)S(1)} collective-permute-done((bf16[1024,1024]{1,0:T(8,128)(2,1)}, bf16[1024,1024]{1,0:T(8,128)(2,1)S(1)}, u32[]{:S(2)}, u32[]{:S(2)}) %collective-permute-start) | collective-permute-done | bytes 2097184 | tf_op jit(solution)/shard_map/ppermute | solution.py:12
  357.6 7.0 %convert_select_fusion.1 = (f32[1024,1024]{1,0:T(8,128)}, f32[1024,1024]{1,0:T(8,128)}) fusion(f32[1024,1024]{1,0:T(8,128)} %get-tuple-element.6, bf16[1024,1024]{1,0:T(8,128)(2,1)S(1)} %collective-permute-done, pred[]{:T(512)S(6)} %eq.38), kind=kLoop, calls=%fused_computation.11 | loop fusion | flops 3145728 | bytes 14680065 | tf_op jit(solution)/shard_map/jit(_where)/select_n | solution.py:68
  364.6 0.0 all-gather.6.cloned.1.call-done
  364.6 10.2 %fusion.8 = bf16[512,1024]{1,0:T(8,128)(2,1)} fusion(bf16[512,4096]{1,0:T(8,128)(2,1)} %bitcast.7, bf16[1,1024,4096]{2,1,0:T(8,128)(2,1)} %all-gather.6.cloned.1.call-done), kind=kOutput, calls=%fused_computation.16 | convolution fusion | flops 4295491584 | bytes 13631488 | tf_op jit(solution)/shard_map/dot_general | solution.py:41
  374.9 7.8 %all-to-all-start.1 = ((bf16[8,64,1024]{2,1,0:T(8,128)(2,1)}), bf16[8,64,1024]{2,1,0:T(8,128)(2,1)S(1)}, u32[]{:S(2)}, u32[]{:S(2)}) async-start(bf16[8,64,1024]{2,1,0:T(8,128)(2,1)} %bitcast.9), calls=%async_computation.1 | async-start | bytes 2097152 | tf_op jit(solution)/shard_map/all_to_all | solution.py:47
  382.7 0.0 copy-start
  382.7 0.0 copy-start.1
  382.7 0.0 copy-start.2
  382.7 33.1 %bitcast_add_fusion = f32[1,1024,2048]{2,1,0:T(8,128)} fusion(f32[1,1024,2048]{2,1,0:T(8,128)} %param.11, f32[1024,1024]{1,0:T(8,128)} %get-tuple-element.6, f32[1024,1024]{1,0:T(8,128)} %get-tuple-element.4, f32[1024,1024]{1,0:T(8,128)} %get-tuple-element.3), kind=kOutput, calls=%fused_computation.5 | convolution fusion | flops 25778192384 | bytes 29360128 | tf_op jit(solution)/shard_map/dot_general | solution.py:74
  415.8 0.0 copy-done
  415.8 0.0 copy-done.1
  415.8 0.0 copy-done.2
  415.8 15.1 %bitcast_add_fusion.1 = f32[1,512,1024]{2,1,0:T(8,128)} fusion(f32[1,512,1024]{2,1,0:T(8,128)S(1)} %copy-done.2, f32[1024,1024]{1,0:T(8,128)S(1)} %copy-done.1, f32[1024,1024]{1,0:T(8,128)S(1)} %copy-done, s32[]{:T(128)S(6)} %select_n.32), kind=kOutput, calls=%fused_computation.13 | convolution fusion | flops 12889620480 | bytes 20971524 | tf_op jit(solution)/shard_map/dot_general | solution.py:86
  430.9 0.0 all-to-all-done.1
  430.9 2.0 gather_fusion
  (3 shorter events, 0.0 us)
Async XLA Ops:
  7.2 85.1 %all-gather.4.cloned.1.call-start = ((), (), s32[]{:S(2)}) async-start(), calls=%async_computation.3 | async-start | bytes 5242880 | tf_op jit(solution)/shard_map/all_gather | solution.py:61
  18.0 50.9 %all-to-all-start = ((bf16[8,64,4096]{2,1,0:T(8,128)(2,1)}), bf16[8,64,4096]{2,1,0:T(8,128)(2,1)}, u32[]{:S(2)}, u32[]{:S(2)}) async-start(bf16[8,64,4096]{2,1,0:T(8,128)(2,1)} %bitcast.34), calls=%async_computation | async-start | bytes 8388608 | tf_op jit(solution)/shard_map/all_to_all | solution.py:32
  23.2 341.4 %all-gather.6.cloned.1.call-start = ((), (), s32[]{:S(2)}) async-start(), calls=%async_computation.4 | async-start | bytes 10485760 | tf_op jit(solution)/shard_map/all_gather | solution.py:43
  82.2 204.6 %all-to-all-start.2 = ((bf16[512,4,1024]{2,0,1:T(8,128)(2,1)}), bf16[512,4,1024]{2,0,1:T(8,128)(2,1)}, u32[]{:S(2)}, u32[]{:S(2)}) async-start(bf16[512,4,1024]{2,0,1:T(8,128)(2,1)} %copy.10), calls=%async_computation.2 | async-start | bytes 8388608 | tf_op jit(solution)/shard_map/all_to_all | solution.py:57
  297.5 60.1 %collective-permute-start = (bf16[1024,1024]{1,0:T(8,128)(2,1)}, bf16[1024,1024]{1,0:T(8,128)(2,1)S(1)}, u32[]{:S(2)}, u32[]{:S(2)}) collective-permute-start(bf16[1024,1024]{1,0:T(8,128)(2,1)} %get-tuple-element.5), channel_id=1, source_target_pairs={{0,8},{8,0},{16,24},{24,16},{1,9},{9,1},{17,25},{25,17},{2,10},{10... | collective-permute-start | bytes 6291464 | tf_op jit(solution)/shard_map/ppermute | solution.py:12
  374.9 56.1 %all-to-all-start.1 = ((bf16[8,64,1024]{2,1,0:T(8,128)(2,1)}), bf16[8,64,1024]{2,1,0:T(8,128)(2,1)S(1)}, u32[]{:S(2)}, u32[]{:S(2)}) async-start(bf16[8,64,1024]{2,1,0:T(8,128)(2,1)} %bitcast.9), calls=%async_computation.1 | async-start | bytes 2097152 | tf_op jit(solution)/shard_map/all_to_all | solution.py:47
  382.7 33.1 %copy-start = (f32[1024,1024]{1,0:T(8,128)S(1)}, f32[1024,1024]{1,0:T(8,128)}, u32[]{:S(2)}) copy-start(f32[1024,1024]{1,0:T(8,128)} %get-tuple-element.3) | copy-start | bytes 12582916
  382.7 33.1 %copy-start.1 = (f32[1024,1024]{1,0:T(8,128)S(1)}, f32[1024,1024]{1,0:T(8,128)}, u32[]{:S(2)}) copy-start(f32[1024,1024]{1,0:T(8,128)} %get-tuple-element.4) | copy-start | bytes 12582916
  382.7 33.1 %copy-start.2 = (f32[1,512,1024]{2,1,0:T(8,128)S(1)}, f32[1,512,1024]{2,1,0:T(8,128)}, u32[]{:S(2)}) copy-start(f32[1,512,1024]{2,1,0:T(8,128)} %param.10) | copy-start | bytes 6291460
Sparse Core Ops, SparseCore 0:
  9.5 82.6 all-gather.3
  93.8 223.5 all-gather.5
where the time goes:
time: 446 us; the launch traced here: 440 us
  waiting for transfers between devices  305 us (68%)
  matrix products  69.1 us (15%)
  local copies, waits for them, and re-layouts  22.6 us (5%)
  starting transfers between devices  18.9 us (4%)
  between operations  14.3 us (3%)
  other arithmetic  9.75 us (2%)
    all_to_all x1, waiting for transfers between devices, local(): lax.all_to_all(arrived, 'dp', split_axis=1, concat_axis=0, tiled=True)  195 us
    ppermute x1, waiting for transfers between devices, swapped(): return lax.ppermute(value, axis, pairs)  60.1 us
    all_to_all x1, waiting for transfers between devices, local(): lax.all_to_all(outgoing.reshape(expert_count, capacity, model_width), 'ex...  44.9 us
    dot_general x1, matrix products, local(): lax.dot_general(own_piece, block_grad, (((1,), (1,)), ((), ())), precisio...  33.1 us
    dot_general x1, matrix products, local(): lax.dot_general(hidden_cols, block_grad, (((0,), (0,)), ((), ())), precis...  15.1 us
    all_to_all x2, local copies, waits for them, and re-layouts, local(): lax.all_to_all(arrived, 'dp', split_axis=1, concat_axis=0, tiled=True)  13.3 us
    dot_general x1, matrix products, local(): lax.dot_general(columns, lax.all_gather(hidden, 'dp', axis=0, tiled=True)...  10.7 us
    dot_general x1, matrix products, local(): lax.dot_general(columns, lax.all_gather(weight[0], 'dp', axis=1, tiled=Tr...  10.2 us
  transfers between devices with their start and end apart: 6, of which 4 were waited for; matrix products, arithmetic and copies ran while one was open for 19% of the time, Pallas kernels for 0%

commit v1 on v0

--- a/solution.py
+++ b/solution.py
@@ -54,7 +54,10 @@
     grad_rows = returned.reshape(slot_count, hidden_width)[target_slots]
     half_width = model_width // group_count
     block_width = 2 * half_width
-    columns_all = lax.all_to_all(arrived, "dp", split_axis=1, concat_axis=0, tiled=True)
+    columns_all = jnp.concatenate(
+        lax.all_to_all(jnp.stack(jnp.split(arrived, lax.axis_size("dp"), axis=1)), "dp", 0, 0),
+        axis=0,
+    )
     columns = columns_all
     own_piece = lax.dot_general(
         columns,

time: 446 us -> 424 us (0.951); the launches traced: 440 us -> 423 us
  local copies, waits for them, and re-layouts: 22.6 us -> 12 us
    all_to_all x1, waiting for transfers between devices: 195 us -> 133 us  [local(): lax.all_to_all(jnp.stack(jnp.split(arrived, lax.axis_size('dp'), axis=1))...]
    all_gather x1, waiting for transfers between devices: 4.23 us -> 39.6 us  [local(): lax.all_gather(hidden, 'dp', axis=0, tiled=True)]
    ppermute x1, waiting for transfers between devices: 60.1 us -> 82.5 us  [swapped(): return lax.ppermute(value, axis, pairs)]
    all_to_all x2 -> x0, local copies, waits for them, and re-layouts: 13.3 us -> none  [local(): lax.all_to_all(arrived, 'dp', split_axis=1, concat_axis=0, tiled=True)]
where the time goes in v1:
time: 424 us; the launch traced here: 423 us
  waiting for transfers between devices  302 us (71%)
  matrix products  68.9 us (16%)
  starting transfers between devices  14.7 us (3%)
  between operations  14.1 us (3%)
  other arithmetic  12.1 us (3%)
  local copies, waits for them, and re-layouts  12 us (3%)
    all_to_all x1, waiting for transfers between devices, local(): lax.all_to_all(jnp.stack(jnp.split(arrived, lax.axis_size('dp'), axis=1))...  133 us
    ppermute x1, waiting for transfers between devices, swapped(): return lax.ppermute(value, axis, pairs)  82.5 us
    all_to_all x1, waiting for transfers between devices, local(): lax.all_to_all(outgoing.reshape(expert_count, capacity, model_width), 'ex...  44.9 us
    all_gather x1, waiting for transfers between devices, local(): lax.all_gather(hidden, 'dp', axis=0, tiled=True)  39.6 us
    dot_general x1, matrix products, local(): lax.dot_general(own_piece, block_grad, (((1,), (1,)), ((), ())), precisio...  32.9 us
    dot_general x1, matrix products, local(): lax.dot_general(hidden_cols, block_grad, (((0,), (0,)), ((), ())), precis...  15.1 us
    dot_general x1, matrix products, local(): lax.dot_general(columns, lax.all_gather(hidden, 'dp', axis=0, tiled=True)...  10.7 us
    dot_general x1, matrix products, local(): lax.dot_general(columns, lax.all_gather(weight[0], 'dp', axis=1, tiled=Tr...  10.2 us
  transfers between devices with their start and end apart: 6, of which 4 were waited for; matrix products, arithmetic and copies ran while one was open for 19% of the time, Pallas kernels for 0%

profile of v1, /device:TPU:1, one launch (start us, length us, event | category | flops | bytes accessed | tf_op | source)
XLA Modules:
  0.0 423.4 jit_solution(742801837169250289)
XLA Ops:
  7.2 0.0 all-gather.4.cloned.1.call-start
  7.2 0.7 all-gather.4.cloned.1.call-update
  7.9 0.7 fusion.15
  8.6 0.6 reduce-window.6
  9.2 0.2 slice_reduce_fusion
  9.4 0.8 fusion.14
  10.2 0.7 compare_select_fusion
  10.9 7.1 %scatter_custom_fusion = bf16[512,4096]{1,0:T(8,128)(2,1)} fusion(s32[256]{0:T(256)S(1)} %bitcast.43, bf16[256,4096]{1,0:T(8,128)(2,1)} %param.6, bf16[]{:T(256)} %constant.14.clone.1), kind=kCustom, calls=%fused_computation.15 | custom fusion | bytes 4194816 | tf_op jit(solution)/shard_map/scatter | solution.py:31
  18.0 5.2 %all-to-all-start = ((bf16[8,64,4096]{2,1,0:T(8,128)(2,1)}), bf16[8,64,4096]{2,1,0:T(8,128)(2,1)}, u32[]{:S(2)}, u32[]{:S(2)}) async-start(bf16[8,64,4096]{2,1,0:T(8,128)(2,1)} %bitcast.40), calls=%async_computation | async-start | bytes 8388608 | tf_op jit(solution)/shard_map/all_to_all | solution.py:32
  23.2 0.0 all-gather.6.cloned.1.call-start
  23.2 0.7 all-gather.6.cloned.1.call-update
  23.9 44.9 %all-to-all-done = bf16[8,64,4096]{2,1,0:T(8,128)(2,1)} async-done(((bf16[8,64,4096]{2,1,0:T(8,128)(2,1)}), bf16[8,64,4096]{2,1,0:T(8,128)(2,1)}, u32[]{:S(2)}, u32[]{:S(2)}) %all-to-all-start) | async-done | bytes 4194336 | tf_op jit(solution)/shard_map/all_to_all | solution.py:32
  68.9 2.6 slice_bitcast_fusion.3
  71.5 2.3 pad_maximum_fusion.3
  73.8 5.3 %all-to-all-start.2 = ((bf16[4,512,1024]{2,1,0:T(8,128)(2,1)}), bf16[4,512,1024]{2,1,0:T(8,128)(2,1)}, u32[]{:S(2)}, u32[]{:S(2)}) async-start(bf16[4,512,1024]{2,1,0:T(8,128)(2,1)} %pad_maximum_fusion.3), calls=%async_computation.2 | async-start | bytes 8388608 | tf_op jit(solution)/shard_map/all_to_all | solution.py:58
  79.1 39.6 %all-gather.4.cloned.1.call-done = bf16[2048,1024]{1,0:T(8,128)(2,1)} async-done(((bf16[512,1024]{1,0:T(8,128)(2,1)}), bf16[2048,1024]{1,0:T(8,128)(2,1)}) %all-gather.4.cloned.1.call-update) | async-done | bytes 4194320 | tf_op jit(solution)/shard_map/all_gather | solution.py:64
  118.8 133.2 %all-to-all-done.2 = bf16[4,512,1024]{2,1,0:T(8,128)(2,1)} async-done(((bf16[4,512,1024]{2,1,0:T(8,128)(2,1)}), bf16[4,512,1024]{2,1,0:T(8,128)(2,1)}, u32[]{:S(2)}, u32[]{:S(2)}) %all-to-all-start.2) | async-done | bytes 4194336 | tf_op jit(solution)/shard_map/all_to_all | solution.py:58
  251.9 10.7 %fusion.19 = (bf16[1024,1024]{1,0:T(8,128)(2,1)}, f32[1024,1024]{1,0:T(8,128)}) fusion(bf16[2048,1024]{1,0:T(8,128)(2,1)} %bitcast.15, bf16[2048,1024]{1,0:T(8,128)(2,1)} %all-gather.4.cloned.1.call-done), kind=kOutput, calls=%fused_computation.34 | convolution fusion | flops 4296015872 | bytes 14680064 | tf_op jit(solution)/shard_map/dot_general | solution.py:62
  262.7 0.0 collective-permute-start
  262.7 82.5 %collective-permute-done = bf16[1024,1024]{1,0:T(8,128)(2,1)S(1)} collective-permute-done((bf16[1024,1024]{1,0:T(8,128)(2,1)}, bf16[1024,1024]{1,0:T(8,128)(2,1)S(1)}, u32[]{:S(2)}, u32[]{:S(2)}) %collective-permute-start) | collective-permute-done | bytes 2097184 | tf_op jit(solution)/shard_map/ppermute | solution.py:12
  345.2 7.0 %convert_select_fusion.1 = (f32[1024,1024]{1,0:T(8,128)}, f32[1024,1024]{1,0:T(8,128)}) fusion(f32[1024,1024]{1,0:T(8,128)} %get-tuple-element.10, bf16[1024,1024]{1,0:T(8,128)(2,1)S(1)} %collective-permute-done, pred[]{:T(512)S(6)} %eq.38), kind=kLoop, calls=%fused_computation.11 | loop fusion | flops 3145728 | bytes 14680065 | tf_op jit(solution)/shard_map/jit(_where)/select_n | solution.py:71
  352.2 0.0 all-gather.6.cloned.1.call-done
  352.2 10.2 %fusion.8 = bf16[512,1024]{1,0:T(8,128)(2,1)} fusion(bf16[512,4096]{1,0:T(8,128)(2,1)} %bitcast.7, bf16[1,1024,4096]{2,1,0:T(8,128)(2,1)} %all-gather.6.cloned.1.call-done), kind=kOutput, calls=%fused_computation.17 | convolution fusion | flops 4295491584 | bytes 13631488 | tf_op jit(solution)/shard_map/dot_general | solution.py:41
  362.5 4.1 all-to-all-start.1
  366.6 0.0 copy-start
  366.6 0.0 copy-start.1
  366.6 0.0 copy-start.2
  366.6 32.9 %bitcast_add_fusion = f32[1,1024,2048]{2,1,0:T(8,128)} fusion(f32[1,1024,2048]{2,1,0:T(8,128)} %param.11, f32[1024,1024]{1,0:T(8,128)} %get-tuple-element.10, f32[1024,1024]{1,0:T(8,128)} %get-tuple-element.4, f32[1024,1024]{1,0:T(8,128)} %get-tuple-element.3), kind=kOutput, calls=%fused_computation.5 | convolution fusion | flops 25778192384 | bytes 29360128 | tf_op jit(solution)/shard_map/dot_general | solution.py:77
  399.5 0.0 copy-done
  399.5 0.0 copy-done.1
  399.5 0.0 copy-done.2
  399.5 15.1 %bitcast_add_fusion.1 = f32[1,512,1024]{2,1,0:T(8,128)} fusion(f32[1,512,1024]{2,1,0:T(8,128)S(1)} %copy-done.2, f32[1024,1024]{1,0:T(8,128)S(1)} %copy-done.1, f32[1024,1024]{1,0:T(8,128)S(1)} %copy-done, s32[]{:T(128)S(6)} %select_n.32), kind=kOutput, calls=%fused_computation.14 | convolution fusion | flops 12889620480 | bytes 20971524 | tf_op jit(solution)/shard_map/dot_general | solution.py:89
  414.6 0.0 all-to-all-done.1
  414.6 2.0 gather_fusion
  (3 shorter events, 0.0 us)
Async XLA Ops:
  7.2 111.6 %all-gather.4.cloned.1.call-start = ((), (), s32[]{:S(2)}) async-start(), calls=%async_computation.3 | async-start | bytes 5242880 | tf_op jit(solution)/shard_map/all_gather | solution.py:64
  18.0 50.9 %all-to-all-start = ((bf16[8,64,4096]{2,1,0:T(8,128)(2,1)}), bf16[8,64,4096]{2,1,0:T(8,128)(2,1)}, u32[]{:S(2)}, u32[]{:S(2)}) async-start(bf16[8,64,4096]{2,1,0:T(8,128)(2,1)} %bitcast.40), calls=%async_computation | async-start | bytes 8388608 | tf_op jit(solution)/shard_map/all_to_all | solution.py:32
  23.2 329.0 %all-gather.6.cloned.1.call-start = ((), (), s32[]{:S(2)}) async-start(), calls=%async_computation.4 | async-start | bytes 10485760 | tf_op jit(solution)/shard_map/all_gather | solution.py:43
  73.8 178.1 %all-to-all-start.2 = ((bf16[4,512,1024]{2,1,0:T(8,128)(2,1)}), bf16[4,512,1024]{2,1,0:T(8,128)(2,1)}, u32[]{:S(2)}, u32[]{:S(2)}) async-start(bf16[4,512,1024]{2,1,0:T(8,128)(2,1)} %pad_maximum_fusion.3), calls=%async_computation.2 | async-start | bytes 8388608 | tf_op jit(solution)/shard_map/all_to_all | solution.py:58
  262.7 82.5 %collective-permute-start = (bf16[1024,1024]{1,0:T(8,128)(2,1)}, bf16[1024,1024]{1,0:T(8,128)(2,1)S(1)}, u32[]{:S(2)}, u32[]{:S(2)}) collective-permute-start(bf16[1024,1024]{1,0:T(8,128)(2,1)} %get-tuple-element.9), channel_id=1, source_target_pairs={{0,8},{8,0},{16,24},{24,16},{1,9},{9,1},{17,25},{25,17},{2,10},{10... | collective-permute-start | bytes 6291464 | tf_op jit(solution)/shard_map/ppermute | solution.py:12
  362.5 52.2 %all-to-all-start.1 = ((bf16[8,64,1024]{2,1,0:T(8,128)(2,1)}), bf16[8,64,1024]{2,1,0:T(8,128)(2,1)S(1)}, u32[]{:S(2)}, u32[]{:S(2)}) async-start(bf16[8,64,1024]{2,1,0:T(8,128)(2,1)} %bitcast.9), calls=%async_computation.1 | async-start | bytes 2097152 | tf_op jit(solution)/shard_map/all_to_all | solution.py:47
  366.6 32.9 %copy-start = (f32[1024,1024]{1,0:T(8,128)S(1)}, f32[1024,1024]{1,0:T(8,128)}, u32[]{:S(2)}) copy-start(f32[1024,1024]{1,0:T(8,128)} %get-tuple-element.3) | copy-start | bytes 12582916
  366.6 32.9 %copy-start.1 = (f32[1024,1024]{1,0:T(8,128)S(1)}, f32[1024,1024]{1,0:T(8,128)}, u32[]{:S(2)}) copy-start(f32[1024,1024]{1,0:T(8,128)} %get-tuple-element.4) | copy-start | bytes 12582916
  366.6 32.9 %copy-start.2 = (f32[1,512,1024]{2,1,0:T(8,128)S(1)}, f32[1,512,1024]{2,1,0:T(8,128)}, u32[]{:S(2)}) copy-start(f32[1,512,1024]{2,1,0:T(8,128)} %param.10) | copy-start | bytes 6291460
Sparse Core Ops, SparseCore 0:
  9.5 109.1 all-gather.3
  120.3 209.8 all-gather.5
